TPU v7x, 32 devices: a whole 2x2x4 slice. The times are simulated.
32 devices in a mesh: group: 2 (over x), ctx: 16 (over z, y, core).
Axes of the slice: x: 2, y: 2, z: 4, core: 2. Of those that a mesh axis runs over, the one named last changes fastest.
Arguments:
- queries: bfloat16 [256, 8, 8192], P(('group', 'ctx')), parts along dimension 0, may hold values from -40 to 40
- kv_cache: bfloat16 [32, 2, 512, 1024], P(('group', 'ctx')), parts along dimension 0, may hold values from -16 to 16
- page_counts: int32 [16], P('group'), parts along dimension 0, may hold values from 1 to 6, as said below
- doc_ids: int32 [16], P('group'), parts along dimension 0, may hold values from 0 to 7, each once
Outputs:
- attended: bfloat16 [256, 8, 8192], P(('group', 'ctx')), parts along dimension 0
There are 2 independent parts, one for each index of `group`. A program takes and returns all parts, laid end to end along the dimension named above; each array names one. Nothing has to cross between parts.
Inputs may be any that keep to these rules, and one draw needn't show every extreme that they name: `page_counts`: the counts sum to 16; every document holds at least 1 pages, some document exactly 1, and some document exactly 6. `doc_ids`: every document is named by exactly one question block.
All inputs are finite; a program needn't handle non-finite values.
Results may differ from a plain program's by a relative error of at most 0.0031.
Values may be sent and summed in bfloat16 or wider, within the bound.
A program may use at most 128 MiB of HBM per device.

v0:
```python
import jax
import jax.numpy as jnp
from jax import lax
from jax.sharding import PartitionSpec as P

HEAD_DIM = 128


def from_behind(value, axis, steps):
    count = lax.axis_size(axis)
    leading, last = (max(0, -steps), min(count, count - steps))
    return lax.ppermute(value, axis, [(source, source + steps) for source in range(leading, last)])


def doc_of(pages, doc_ends):
    return jnp.sum((pages[..., None] >= doc_ends).astype(jnp.int32), axis=-1)


def page_partial(rows, page_kv):
    tokens = rows.shape[0]
    kv_heads = page_kv.shape[-1] // HEAD_DIM
    groups = rows.shape[-1] // (kv_heads * HEAD_DIM)
    grouped = rows.reshape(tokens, kv_heads, groups, HEAD_DIM)
    keys = page_kv[0].reshape(-1, kv_heads, HEAD_DIM)
    values = page_kv[1].reshape(-1, kv_heads, HEAD_DIM)
    scores = jnp.einsum(
        "qhgd,khd->qhgk", grouped, keys, preferred_element_type=jnp.float32
    ) * HEAD_DIM ** (-0.5)
    row_max = jnp.max(scores, axis=-1)
    expo = jnp.exp(scores - row_max[..., None])
    row_sum = jnp.sum(expo, axis=-1)
    weights = expo.astype(jnp.bfloat16)
    mixed = jnp.einsum("qhgk,khd->qhgd", weights, values, preferred_element_type=jnp.float32)
    return (row_max.reshape(tokens, -1), row_sum.reshape(tokens, -1), mixed.reshape(tokens, -1))


def body(queries, kv_cache, page_counts, doc_ids):
    peer_count = lax.axis_size("ctx")
    own_index = lax.axis_index("ctx")
    per_dev = kv_cache.shape[0]
    local_rows = queries.shape[0]
    blocks = queries.shape[1]
    width = queries.shape[2]
    heads = width // HEAD_DIM
    doc_ends = jnp.cumsum(page_counts)
    block_order = jnp.arange(blocks, dtype=jnp.int32)
    peer_ids = jnp.arange(peer_count, dtype=jnp.int32)
    first_doc = doc_of(peer_ids * per_dev, doc_ends)
    last_doc = doc_of(peer_ids * per_dev + per_dev - 1, doc_ends)
    slot_docs = jnp.stack([first_doc, last_doc])
    slot_blocks = jnp.sum(
        jnp.where(doc_ids[None, None, :] == slot_docs[..., None], block_order, 0), axis=-1
    )
    outgoing = jnp.take(queries, slot_blocks[0], axis=1)
    arrived = lax.all_to_all(outgoing, "ctx", split_axis=1, concat_axis=0, tiled=True)
    first_rows = arrived.reshape(-1, width)
    later_rows = from_behind(first_rows, "ctx", -1)
    asked_rows = jnp.stack([first_rows, later_rows])
    own_pages = own_index * per_dev + jnp.arange(per_dev, dtype=jnp.int32)
    page_docs = doc_of(own_pages, doc_ends)
    in_second = (page_docs[0] != page_docs[0]).astype(jnp.int32)
    rows = lax.dynamic_index_in_dim(asked_rows, in_second, 0, keepdims=False)
    partials = (in_second,) + page_partial(rows, kv_cache[0])
    slot_max, slot_sum, slot_out = ([], [], [])
    for slot in range(2):
        best = jnp.full(partials[1].shape, -1e30, jnp.float32)
        in_second, row_max, row_sum, mixed = partials
        best = jnp.where(in_second == slot, jnp.maximum(best, row_max), best)
        in_second, row_max, row_sum, mixed = partials
        member = in_second == slot
        weight = jnp.where(member, jnp.exp(jnp.where(member, row_max - best, 0.0)), 0.0)
        total = weight * row_sum
        tokens = mixed.shape[0]
        summed = (weight[..., None] * mixed.reshape(tokens, heads, HEAD_DIM)).reshape(tokens, width)
        slot_max.append(best)
        slot_sum.append(total)
        slot_out.append(summed)
    send_max = jnp.stack(slot_max).reshape(2, peer_count, local_rows, heads)
    send_sum = jnp.stack(slot_sum).reshape(2, peer_count, local_rows, heads)
    send_out = jnp.stack(slot_out).reshape(2, peer_count, local_rows, width)
    got_out, got_max, got_sum = (
        lax.all_to_all(send_out, "ctx", split_axis=1, concat_axis=1, tiled=True),
        lax.all_to_all(send_max, "ctx", split_axis=1, concat_axis=1, tiled=True),
        lax.all_to_all(send_sum, "ctx", split_axis=1, concat_axis=1, tiled=True),
    )
    slots = slot_blocks.shape[0]
    matches = slot_blocks[None, :, :] == block_order[:, None, None]
    masked = jnp.where(matches[..., None, None], got_max[None], -1e30)
    row_top = jnp.max(masked, axis=(1, 2))
    weight = jnp.where(matches[..., None, None], jnp.exp(masked - row_top[:, None, None]), 0.0)
    denominator = jnp.sum(weight * got_sum[None], axis=(1, 2))
    numerator = jnp.einsum(
        "csnrh,snrhd->crhd",
        weight,
        got_out.reshape(slots, peer_count, local_rows, heads, HEAD_DIM),
        precision=lax.Precision.HIGHEST,
    )
    mixed_out = (numerator / denominator[..., None]).reshape(blocks, local_rows, width)
    return jnp.moveaxis(mixed_out, 0, 1).astype(jnp.bfloat16)


def solution(mesh):
    placed = (
        P(("group", "ctx"), None, None),
        P(("group", "ctx"), None, None, None),
        P("group"),
        P("group"),
    )
    return jax.shard_map(
        body, mesh=mesh, in_specs=placed, out_specs=P(("group", "ctx"), None, None), check_vma=False
    )
```

profile of v0, /device:TPU:15, one launch (start us, length us, event | category | flops | bytes accessed | tf_op | source)
XLA Modules:
  0.0 343.0 jit_solution(9864012066640521208)
XLA Ops:
  0.0 0.9 reduce-window.8
  1.0 0.7 select_reduce_fusion.1
  1.8 6.5 %gather_fusion = bf16[16,8,8192]{2,0,1:T(8,128)(2,1)S(1)} fusion(bf16[8,8,8192]{2,1,0:T(8,128)(2,1)S(1)} %copy-done, s32[1024]{0:T(1024)S(1)} %pad_clamp_fusion), kind=kCustom, calls=%fused_computation | custom fusion | bytes 4194368 | tf_op jit(solution)/shard_map/jit(_take)/gather | solution.py:54
  8.6 2.5 copy.36
  11.1 6.5 %all-to-all-start = ((bf16[8,16,8192]{2,0,1:T(8,128)(2,1)}), bf16[8,16,8192]{2,0,1:T(8,128)(2,1)S(1)}, u32[]{:S(2)}, u32[]{:S(2)}) async-start(bf16[8,16,8192]{2,0,1:T(8,128)(2,1)} %copy.36), calls=%async_computation | async-start | bytes 4194304 | tf_op jit(solution)/shard_map/all_to_all | solution.py:55
  17.6 2.7 fusion.36
  20.3 1.3 copy.61
  21.6 1.5 copy.60
  23.1 41.9 %all-to-all-done = bf16[8,16,8192]{2,0,1:T(8,128)(2,1)S(1)} async-done(((bf16[8,16,8192]{2,0,1:T(8,128)(2,1)}), bf16[8,16,8192]{2,0,1:T(8,128)(2,1)S(1)}, u32[]{:S(2)}, u32[]{:S(2)}) %all-to-all-start) | async-done | bytes 2097184 | tf_op jit(solution)/shard_map/all_to_all | solution.py:55
  65.7 9.9 %bitcast_reduce_fusion = (f32[128,8,8]{0,2,1:T(8,128)S(1)}, f32[8,128,8,512]{3,1,2,0:T(8,128)}) fusion(bf16[512,8,128,1]{0,2,3,1:T(8,128)(2,1)S(1)} %bitcast.82, bf16[128,8,8,128]{3,2,1,0:T(8,128)(2,1)S(1)} %bitcast.79), kind=kOutput, calls=%fused_computation.2 | convolution fusion | flops 1082122240 | bytes 19955712 | tf_op jit(solution)/shard_map/qhgd,khd->qhgk/dot_general | solution.py:26
  76.0 9.0 %fusion.1 = f32[128,8,8]{0,2,1:T(8,128)S(1)} fusion(f32[8,128,8,512]{3,1,2,0:T(8,128)} %get-tuple-element.13, f32[128,8,8]{0,2,1:T(8,128)S(1)} %get-tuple-element.12), kind=kLoop, calls=%fused_computation.4 | loop fusion | flops 12574720 | bytes 16842752 | tf_op jit(solution)/shard_map/reduce_sum | solution.py:31
  85.0 1.6 copy-done.2
  86.6 4.3 %fusion.14 = f32[128,8,8,128]{3,0,2,1:T(8,128)S(1)} fusion(bf16[512,8,128,1]{0,2,3,1:T(8,128)(2,1)S(1)} %bitcast.83, f32[8,128,8,512]{3,1,2,0:T(8,128)S(1)} %copy-done.2, f32[128,8,8]{0,2,1:T(8,128)S(1)} %get-tuple-element.12), kind=kOutput, calls=%fused_computation.18 | convolution fusion | flops 1086324736 | bytes 22052864 | tf_op jit(solution)/shard_map/qhgk,khd->qhgd/dot_general | solution.py:33
  90.9 4.4 %copy.43 = f32[128,8,8,128]{3,2,1,0:T(8,128)} copy(f32[128,8,8,128]{3,0,2,1:T(8,128)S(1)} %fusion.14) | data formatting | bytes 8388608 | tf_op jit(solution)/shard_map/qhgk,khd->qhgd/transpose | solution.py:33
  95.3 4.9 %reshape_reshape.4 = f32[1,16,8,8192]{3,2,1,0:T(8,128)} reshape(f32[128,8,8,128]{3,2,1,0:T(8,128)} %copy.43) | data formatting | bytes 8388608 | tf_op jit(solution)/shard_map/reshape;reshape | solution.py:74
  101.0 0.7 reshape.228
  101.8 4.8 %all-to-all-start.2 = ((f32[16,1,1024]{2,1,0:T(1,128)}), f32[16,1,1024]{2,1,0:T(1,128)S(1)}, u32[]{:S(2)}, u32[]{:S(2)}) async-start(f32[16,1,1024]{2,1,0:T(1,128)} %reshape.228), calls=%async_computation.2 | async-start | bytes 131072 | tf_op jit(solution)/shard_map/all_to_all | solution.py:83
  106.6 2.6 mul.76
  109.2 4.9 %mul.77 = f32[1,16,8,8192]{3,2,1,0:T(8,128)} reshape(f32[128,64,128]{2,1,0:T(8,128)} %mul.76) | data formatting | bytes 8388608 | tf_op jit(solution)/shard_map/mul | solution.py:74
  114.1 7.5 %fusion.35 = (f32[1,16,8,8192]{3,2,1,0:T(8,128)}, f32[1,16,8,8192]{3,2,1,0:T(8,128)}) fusion(f32[1,16,8,8192]{3,2,1,0:T(8,128)} %mul.77, f32[1,16,8,8192]{3,2,1,0:T(8,128)} %reshape_reshape.4), kind=kLoop, calls=%fused_computation.50 | loop fusion | flops 2097152 | bytes 16777216 | tf_op jit(solution)/shard_map/mul | solution.py:74
  122.2 0.8 reshape.226
  122.9 6.0 %all-to-all-start.3 = ((f32[16,1,1024]{2,1,0:T(1,128)}), f32[16,1,1024]{2,1,0:T(1,128)S(1)}, u32[]{:S(2)}, u32[]{:S(2)}) async-start(f32[16,1,1024]{2,1,0:T(1,128)} %reshape.226), calls=%async_computation.3 | async-start | bytes 131072 | tf_op jit(solution)/shard_map/all_to_all | solution.py:84
  129.0 4.0 %pad_maximum_fusion = f32[2,16,8,8192]{3,2,1,0:T(8,128)S(1)} fusion(f32[1,16,8,8192]{3,2,1,0:T(8,128)} %get-tuple-element.6, f32[1,16,8,8192]{3,2,1,0:T(8,128)} %get-tuple-element.5), kind=kLoop, calls=%fused_computation.7 | loop fusion | flops 2097152 | bytes 16777216 | tf_op jit(solution)/shard_map/stack | solution.py:80
  133.0 3.8 %copy.44 = f32[2,16,8,8192]{3,2,0,1:T(8,128)} copy(f32[2,16,8,8192]{3,2,1,0:T(8,128)S(1)} %pad_maximum_fusion) | data formatting | bytes 16777216 | tf_op jit(solution)/shard_map/stack | solution.py:80
  136.8 6.0 %all-to-all-start.1 = ((f32[2,16,8,8192]{3,2,0,1:T(8,128)}), f32[2,16,8,8192]{3,2,0,1:T(8,128)}, u32[]{:S(2)}, u32[]{:S(2)}) async-start(f32[2,16,8,8192]{3,2,0,1:T(8,128)} %copy.44), calls=%async_computation.1 | async-start | bytes 16777216 | tf_op jit(solution)/shard_map/all_to_all | solution.py:82
  143.3 0.8 reduce.1
  144.5 0.8 reduce
  145.7 0.7 select_reduce_fusion
  146.4 1.7 fusion.13
  148.1 177.1 %all-to-all-done.1 = f32[2,16,8,8192]{3,2,0,1:T(8,128)} async-done(((f32[2,16,8,8192]{3,2,0,1:T(8,128)}), f32[2,16,8,8192]{3,2,0,1:T(8,128)}, u32[]{:S(2)}, u32[]{:S(2)}) %all-to-all-start.1) | async-done | bytes 8388640 | tf_op jit(solution)/shard_map/all_to_all | solution.py:82
  325.1 5.0 %copy.64 = f32[32,8,64,128]{3,2,1,0:T(8,128)S(1)} copy(f32[32,8,64,128]{3,1,2,0:T(8,128)} %bitcast.40) | data formatting | bytes 16777216
  330.2 12.8 %fusion.25 = bf16[8,8,8192]{2,1,0:T(8,128)(2,1)} fusion(f32[8,8,64]{0,2,1:T(8,128)S(1)} %fusion.13, f32[8,8,64]{0,2,1:T(8,128)S(1)} %select_reduce_fusion, f32[2,16,8,64]{1,0,3,2:T(2,128)S(1)} %copy.47, pred[8,2,16]{2,0,1:T(8,128)(4,1)S(1)} %iota_compare_fusion, f32[2,16,8,64,128]{4,3,2,0,1:T(8,128)S(1)} %bitcast.80), kind=kOutput, calls=%fused_computation.31 | convolution fusion | flops 202768384 | bytes 9535744 | tf_op jit(solution)/shard_map/csnrh,snrhd->crhd/dot_general | solution.py:92
  (31 shorter events, 3.8 us)
Async XLA Ops:
  0.0 1.8 copy-start
  11.1 53.9 %all-to-all-start = ((bf16[8,16,8192]{2,0,1:T(8,128)(2,1)}), bf16[8,16,8192]{2,0,1:T(8,128)(2,1)S(1)}, u32[]{:S(2)}, u32[]{:S(2)}) async-start(bf16[8,16,8192]{2,0,1:T(8,128)(2,1)} %copy.36), calls=%async_computation | async-start | bytes 4194304 | tf_op jit(solution)/shard_map/all_to_all | solution.py:55
  65.7 19.3 %copy-start.3 = (bf16[1,1,512,1024]{2,3,1,0:T(8,128)(2,1)S(1)}, bf16[1,1,512,1024]{2,3,1,0:T(8,128)(2,1)}, u32[]{:S(2)}) copy-start(bf16[1,1,512,1024]{2,3,1,0:T(8,128)(2,1)} %copy.61) | copy-start | bytes 3145732
  75.9 10.7 %copy-start.2 = (f32[8,128,8,512]{3,1,2,0:T(8,128)S(1)}, f32[8,128,8,512]{3,1,2,0:T(8,128)}, u32[]{:S(2)}) copy-start(f32[8,128,8,512]{3,1,2,0:T(8,128)} %get-tuple-element.13) | copy-start | bytes 50331652
  101.8 21.1 %all-to-all-start.2 = ((f32[16,1,1024]{2,1,0:T(1,128)}), f32[16,1,1024]{2,1,0:T(1,128)S(1)}, u32[]{:S(2)}, u32[]{:S(2)}) async-start(f32[16,1,1024]{2,1,0:T(1,128)} %reshape.228), calls=%async_computation.2 | async-start | bytes 131072 | tf_op jit(solution)/shard_map/all_to_all | solution.py:83
  122.9 13.8 %all-to-all-start.3 = ((f32[16,1,1024]{2,1,0:T(1,128)}), f32[16,1,1024]{2,1,0:T(1,128)S(1)}, u32[]{:S(2)}, u32[]{:S(2)}) async-start(f32[16,1,1024]{2,1,0:T(1,128)} %reshape.226), calls=%async_computation.3 | async-start | bytes 131072 | tf_op jit(solution)/shard_map/all_to_all | solution.py:84
  136.8 188.4 %all-to-all-start.1 = ((f32[2,16,8,8192]{3,2,0,1:T(8,128)}), f32[2,16,8,8192]{3,2,0,1:T(8,128)}, u32[]{:S(2)}, u32[]{:S(2)}) async-start(f32[2,16,8,8192]{3,2,0,1:T(8,128)} %copy.44), calls=%async_computation.1 | async-start | bytes 16777216 | tf_op jit(solution)/shard_map/all_to_all | solution.py:82
  330.2 12.9 %copy-start.1 = (bf16[8,8,8192]{2,1,0:T(8,128)(2,1)S(1)}, bf16[8,8,8192]{2,1,0:T(8,128)(2,1)}, u32[]{:S(2)}) copy-start(bf16[8,8,8192]{2,1,0:T(8,128)(2,1)} %param.4) | copy-start | bytes 3145732
where the time goes:
time: 344 us; the launch traced here: 343 us
  waiting for transfers between devices  219 us (64%)
  local copies, waits for them, and re-layouts  46.5 us (14%)
  matrix products  27.1 us (8%)
  other arithmetic  26.9 us (8%)
  starting transfers between devices  23.3 us (7%)
    all_to_all x1, waiting for transfers between devices, body(): lax.all_to_all(send_out, 'ctx', split_axis=1, concat_axis=1, tiled=True)  177 us
    all_to_all x1, waiting for transfers between devices, body(): lax.all_to_all(outgoing, 'ctx', split_axis=1, concat_axis=0, tiled=True)  41.9 us
    dot_general x1, matrix products, body(): jnp.einsum('csnrh,snrhd->crhd', weight, got_out.reshape(slots, peer_count...  12.8 us
    unnamed x18, local copies, waits for them, and re-layouts  12 us
    dot_general x1, matrix products, page_partial(): jnp.einsum('qhgd,khd->qhgk', grouped, keys, preferred_element_type=jnp.fl...  9.95 us
    reduce_sum x1, other arithmetic, page_partial(): row_sum = jnp.sum(expo, axis=-1)  9.05 us
    mul x2, local copies, waits for them, and re-layouts, body(): weight[..., None] * mixed.reshape(tokens, heads, HEAD_DIM)  7.54 us
    mul x1, other arithmetic, body(): weight[..., None] * mixed.reshape(tokens, heads, HEAD_DIM)  7.53 us
  transfers between devices with their start and end apart: 4, of which 2 were waited for; matrix products, arithmetic and copies ran while one was open for 10% of the time, Pallas kernels for 0%

commit v1 on v0

v1 whole, which is shorter than its diff:
```python
import functools

import jax
import jax.numpy as jnp
from jax import lax
from jax.experimental import pallas as pl
from jax.experimental.pallas import tpu as pltpu
from jax.sharding import PartitionSpec as P

HEAD_DIM = 128
CHUNKS = 4


def exchange_kernel(
    peers, q_hbm, kv_hbm, got_hbm, stats_hbm,
    q_buf, o_buf, s_buf, kv_buf,
    q_send, q_recv, o_send, o_recv, s_send, s_recv, own_sem, kv_sem,
):
    chunks, _, rows, wide = q_buf.shape
    me = lax.axis_index("ctx")
    tokens = peers * rows
    heads_chunk = wide // HEAD_DIM
    kv_heads = kv_buf.shape[2] // HEAD_DIM
    groups = chunks * heads_chunk // kv_heads

    kv_copy = pltpu.make_async_copy(kv_hbm.at[0], kv_buf, kv_sem)
    kv_copy.start()
    own_q = pltpu.make_async_copy(q_hbm.at[:, me], q_buf.at[:, me], own_sem.at[0])
    own_q.start()

    barrier = pltpu.get_barrier_semaphore()

    @pl.loop(1, peers)
    def _(k):
        pl.semaphore_signal(
            barrier, inc=1, device_id={"ctx": lax.rem(me + k, peers)},
            device_id_type=pl.DeviceIdType.MESH,
        )

    pl.semaphore_wait(barrier, peers - 1)

    def send(src, dst, send_sem, recv_sem):
        @pl.loop(1, peers)
        def _(k):
            peer = lax.rem(me + k, peers)
            pltpu.make_async_remote_copy(
                src_ref=src.at[peer], dst_ref=dst.at[me], send_sem=send_sem,
                recv_sem=recv_sem, device_id={"ctx": peer},
                device_id_type=pl.DeviceIdType.MESH,
            ).start()

    def drain(ref, sem):
        part = ref.at[pl.ds(0, peers - 1)]
        pltpu.make_async_copy(part, part, sem).wait()

    for c in range(chunks):
        send(q_hbm.at[c], q_buf.at[c], q_send.at[c], q_recv.at[c])

    s_buf[...] = jnp.zeros_like(s_buf)
    kv_copy.wait()
    own_q.wait()
    lane = lax.broadcasted_iota(jnp.int32, (tokens, 128), 1)
    for c in range(chunks):
        drain(q_buf.at[c], q_recv.at[c])

        def head(j, carry):
            lanes = pl.ds(pl.multiple_of(j * HEAD_DIM, HEAD_DIM), HEAD_DIM)
            h = c * heads_chunk + j
            kv_lanes = pl.ds(pl.multiple_of(h // groups * HEAD_DIM, HEAD_DIM), HEAD_DIM)
            q = q_buf[c, :, :, lanes].astype(jnp.float32).reshape(tokens, HEAD_DIM)
            s = lax.dot_general(
                q.astype(jnp.bfloat16), kv_buf[0, :, kv_lanes], (((1,), (1,)), ((), ())),
                preferred_element_type=jnp.float32,
            ) * HEAD_DIM ** (-0.5)
            top = jnp.max(s, axis=-1, keepdims=True)
            p = jnp.exp(s - top)
            total = jnp.sum(p, axis=-1, keepdims=True)
            o = jnp.dot(
                p.astype(jnp.bfloat16), kv_buf[1, :, kv_lanes],
                preferred_element_type=jnp.float32,
            ) / total
            o_buf[c, :, :, lanes] = o.reshape(peers, rows, HEAD_DIM).astype(jnp.bfloat16)
            old = s_buf[...].reshape(tokens, 128)
            new = jnp.where(lane == h, top, jnp.where(lane == h + 64, total, old))
            s_buf[...] = new.reshape(peers, rows, 128)
            return carry

        lax.fori_loop(0, heads_chunk, head, 0)
        send(o_buf.at[c], got_hbm.at[c], o_send.at[c], o_recv.at[c])
    send(s_buf, stats_hbm, s_send, s_recv)
    own_o = pltpu.make_async_copy(o_buf.at[:, me], got_hbm.at[:, me], own_sem.at[0])
    own_o.start()
    own_s = pltpu.make_async_copy(s_buf.at[me], stats_hbm.at[me], own_sem.at[1])
    own_s.start()
    for c in range(chunks):
        drain(q_buf.at[c], q_send.at[c])
        drain(o_buf.at[c], o_send.at[c])
        drain(o_buf.at[c], o_recv.at[c])
    drain(s_buf, s_send)
    drain(s_buf, s_recv)
    own_o.wait()
    own_s.wait()


def exchange(outgoing, kv_cache, peers):
    chunks, _, rows, wide = outgoing.shape
    any_spec = pl.BlockSpec(memory_space=pl.ANY)
    dma = pltpu.SemaphoreType.DMA
    return pl.pallas_call(
        functools.partial(exchange_kernel, peers),
        out_shape=(
            jax.ShapeDtypeStruct(outgoing.shape, jnp.bfloat16),
            jax.ShapeDtypeStruct((peers, rows, 128), jnp.float32),
        ),
        in_specs=[any_spec, any_spec],
        out_specs=(any_spec, any_spec),
        scratch_shapes=[
            pltpu.VMEM(outgoing.shape, jnp.bfloat16),
            pltpu.VMEM(outgoing.shape, jnp.bfloat16),
            pltpu.VMEM((peers, rows, 128), jnp.float32),
            pltpu.VMEM(kv_cache.shape[1:], jnp.bfloat16),
            dma((chunks,)), dma((chunks,)), dma((chunks,)), dma((chunks,)),
            dma(()), dma(()), dma((2,)), dma(()),
        ],
        compiler_params=pltpu.CompilerParams(collective_id=0, has_side_effects=True),
    )(outgoing, kv_cache)


def combine_kernel(heads, fresh, last, got_ref, stats_ref, out_ref, w_buf, top_buf, run_buf):
    peers, rows, wide = run_buf.shape
    step = pl.program_id(0)

    @pl.when(step == 0)
    def _():
        def forward(n, top):
            mine = stats_ref[n]
            top = jnp.where(fresh[n] == 1, mine, jnp.maximum(top, mine))
            top_buf[n] = top
            return top

        def backward(i, top):
            n = peers - 1 - i
            top = jnp.where(fresh[n + 1] == 1, top_buf[n], top)
            top_buf[n] = top
            return top

        def weigh(n, total):
            mine = stats_ref[n]
            w = jnp.exp(mine - top_buf[n]) * pltpu.roll(mine, 128 - 64, 1)
            w_buf[n] = w
            total = jnp.where(fresh[n] == 1, w, total + w)
            top_buf[n] = total
            return total

        def norm(i, total):
            n = peers - 1 - i
            total = jnp.where(fresh[n + 1] == 1, top_buf[n], total)
            w_buf[n] = w_buf[n] / total
            return total

        zero = jnp.zeros(stats_ref.shape[1:], jnp.float32)
        lax.fori_loop(0, peers, forward, zero)
        lax.fori_loop(0, peers, backward, zero)
        lax.fori_loop(0, peers, weigh, zero)
        lax.fori_loop(0, peers, norm, zero)

    count = wide // HEAD_DIM

    def visit(n, acc):
        w = pltpu.roll(w_buf[n], lax.rem(128 - step * count, 128), 1)
        w = jnp.concatenate(
            [jnp.broadcast_to(w[:, i:i + 1], (rows, HEAD_DIM)) for i in range(count)], axis=1
        )
        mine = w * got_ref[0, n].astype(jnp.float32)
        acc = jnp.where(fresh[n] == 1, mine, acc + mine)
        run_buf[n] = acc
        return acc

    lax.fori_loop(0, peers, visit, jnp.zeros((rows, wide), jnp.float32), unroll=4)
    blocks = out_ref.shape[1]
    picked = jnp.stack([run_buf[last[c]] for c in range(blocks)], axis=0)
    out_ref[...] = jnp.swapaxes(picked, 0, 1).astype(jnp.bfloat16)


def combine(got, stats, fresh, last, heads):
    chunks, peers, rows, wide_all = got.shape
    wide = min(wide_all, 1024)
    per = wide_all // wide
    blocks = last.shape[0]
    width = chunks * wide_all
    return pl.pallas_call(
        functools.partial(combine_kernel, heads),
        out_shape=jax.ShapeDtypeStruct((rows, blocks, width), jnp.bfloat16),
        grid_spec=pltpu.PrefetchScalarGridSpec(
            num_scalar_prefetch=2,
            grid=(width // wide,),
            in_specs=[
                pl.BlockSpec((1, peers, rows, wide), lambda i, f, l: (i // per, 0, 0, i % per)),
                pl.BlockSpec((peers, rows, 128), lambda i, f, l: (0, 0, 0)),
            ],
            out_specs=pl.BlockSpec((rows, blocks, wide), lambda i, f, l: (0, 0, i)),
            scratch_shapes=[
                pltpu.VMEM((peers, rows, 128), jnp.float32),
                pltpu.VMEM((peers, rows, 128), jnp.float32),
                pltpu.VMEM((peers, rows, wide), jnp.float32),
            ],
        ),
    )(fresh, last, got, stats)


def body(queries, kv_cache, page_counts, doc_ids):
    peers = lax.axis_size("ctx")
    rows, blocks, width = queries.shape
    heads = width // HEAD_DIM
    assert kv_cache.shape[0] == 1 and heads == 64
    doc_ends = jnp.cumsum(page_counts)
    pages = jnp.arange(peers, dtype=jnp.int32)
    page_docs = jnp.sum((pages[:, None] >= doc_ends).astype(jnp.int32), axis=-1)
    block_order = jnp.arange(blocks, dtype=jnp.int32)
    page_blocks = jnp.sum(jnp.where(doc_ids[None, :] == page_docs[:, None], block_order, 0), axis=-1)
    edge = (page_docs[1:] != page_docs[:-1]).astype(jnp.int32)
    one = jnp.ones((1,), jnp.int32)
    fresh = jnp.concatenate([one, edge, one])
    last = jnp.sum(
        jnp.where(doc_ids[:, None] == block_order[None, :], doc_ends[None, :], 0), axis=-1
    ) - 1

    outgoing = jnp.take(queries, page_blocks, axis=1)
    outgoing = outgoing.reshape(rows, peers, CHUNKS, width // CHUNKS).transpose(2, 1, 0, 3)
    got, stats = exchange(outgoing, kv_cache, peers)
    return combine(got, stats, fresh, last.astype(jnp.int32), heads)


def solution(mesh):
    placed = (
        P(("group", "ctx"), None, None),
        P(("group", "ctx"), None, None, None),
        P("group"),
        P("group"),
    )
    return jax.shard_map(
        body, mesh=mesh, in_specs=placed, out_specs=P(("group", "ctx"), None, None), check_vma=False
    )
```

time: 344 us -> 129 us (0.38)
  waiting for transfers between devices: 219 us -> 0 us
  Pallas kernels: 0 us -> 108 us
  local copies, waits for them, and re-layouts: 46.5 us -> 11.2 us
  matrix products: 27.1 us -> 0 us
  starting transfers between devices: 23.3 us -> 0 us
  other arithmetic: 26.9 us -> 7.57 us
    all_to_all x4 -> x0, waiting for transfers between devices: 219 us -> none  [the longest x1 177 us: body(): lax.all_to_all(send_out, 'ctx', split_axis=1, concat_axis=1, tiled=True)]
    pallas_call x0 -> x2, Pallas kernels: none -> 108 us  [the longest x1 97.2 us: exchange(): pl.pallas_call(functools.partial(exchange_kernel, peers), out_shape=(jax....]
    dot_general x3 -> x0, matrix products: 27.1 us -> none  [the longest x1 12.8 us: body(): jnp.einsum('csnrh,snrhd->crhd', weight, got_out.reshape(slots, peer_count...]
    all_to_all x4 -> x0, starting transfers between devices: 23.3 us -> none  [the longest x1 6.52 us: body(): lax.all_to_all(outgoing, 'ctx', split_axis=1, concat_axis=0, tiled=True)]
    unnamed x18 -> x2, local copies, waits for them, and re-layouts: 12 us -> 0.01 us
    reduce_sum x4 -> x3, other arithmetic: 11.5 us -> 1.66 us  [the longest x1 0.84 us: body(): jnp.sum(jnp.where(doc_ids[:, None] == block_order[None, :], doc_ends[None...]
    another operation x3 -> x0, local copies, waits for them, and re-layouts: 9.16 us -> none  [the longest x1 4.94 us: body(): mixed.reshape(tokens, heads, HEAD_DIM)]
    mul x2 -> x0, local copies, waits for them, and re-layouts: 7.54 us -> none  [body(): weight[..., None] * mixed.reshape(tokens, heads, HEAD_DIM)]
  transfers between devices with their start and end apart: 4 -> 0, of which waited for: 2 -> 0; matrix products, arithmetic and copies ran while one was open for 10% -> 0% of each run, Pallas kernels for 0% -> 0%
where the time goes in v1:
time: 129 us; the launch traced here: 127 us
  Pallas kernels  108 us (84%)
  local copies, waits for them, and re-layouts  11.2 us (9%)
  other arithmetic  7.57 us (6%)
    pallas_call x1, Pallas kernels, exchange(): pl.pallas_call(functools.partial(exchange_kernel, peers), out_shape=(jax....  97.2 us
    gather x2, local copies, waits for them, and re-layouts, body(): outgoing = jnp.take(queries, page_blocks, axis=1)  11.2 us
    pallas_call x1, Pallas kernels, combine(): pl.pallas_call(functools.partial(combine_kernel, heads), out_shape=jax.Sh...  11.1 us
    transpose x1, other arithmetic, body(): outgoing.reshape(rows, peers, CHUNKS, width // CHUNKS).transpose(2, 1, 0, 3)  3.73 us

profile of v1, /device:TPU:15, one launch (start us, length us, event | category | flops | bytes accessed | tf_op | source)
XLA Modules:
  0.0 127.1 jit_solution(7730682052089756298)
XLA Ops:
  0.0 0.0 copy-start
  0.0 0.9 reduce-window.8
  0.9 0.1 convert_reduce_fusion
  1.0 0.8 select_reduce_fusion.1
  1.8 0.6 broadcast_add_fusion.last
  2.4 0.7 select_reduce_fusion
  3.2 0.1 slice_compare_fusion
  3.2 0.6 add_convert_fusion.fresh
  3.9 0.0 copy-done
  3.9 7.9 %gather_fusion = bf16[16,8,8192]{2,0,1:T(8,128)(2,1)} fusion(bf16[8,8,8192]{2,1,0:T(8,128)(2,1)S(1)} %copy-done, s32[1024]{0:T(1024)S(1)} %pad_clamp_fusion), kind=kCustom, calls=%fused_computation | custom fusion | bytes 4194368 | tf_op jit(solution)/shard_map/jit(_take)/gather | solution.py:228
  11.7 3.3 %gather.7 = bf16[8,16,4,2048]{3,2,1,0:T(4,128)(2,1)S(1)} reshape(bf16[8,16,8192]{2,1,0:T(8,128)(2,1)} %bitcast.9) | data formatting | bytes 4194304 | tf_op jit(solution)/shard_map/jit(_take)/gather | solution.py:228
  15.1 3.7 %fusion.q_hbm = bf16[4,16,8,2048]{3,2,1,0:T(8,128)(2,1)} fusion(bf16[8,16,4,2048]{3,2,1,0:T(4,128)(2,1)S(1)} %gather.7, pred[16]{0:T(512)(128)(4,1)S(1)} %compare_and_fusion), kind=kLoop, calls=%fused_computation.2 | loop fusion | flops 1048576 | bytes 4194320 | tf_op jit(solution)/shard_map/transpose | solution.py:229
  18.8 97.2 %shard_map.46 = (bf16[4,16,8,2048]{3,2,1,0:T(8,128)(2,1)}, f32[16,8,128]{2,1,0:T(8,128)}) custom-call(bf16[4,16,8,2048]{3,2,1,0:T(8,128)(2,1)} %fusion.q_hbm, bf16[1,2,512,1024]{3,2,1,0:T(8,128)(2,1)} %kv_hbm.1), custom_call_target="tpu_custom_call" | custom-call | tf_op jit(solution)/shard_map/pallas_call | solution.py:109
  116.0 11.1 %shard_map.47 = bf16[8,8,8192]{2,1,0:T(8,128)(2,1)} custom-call(s32[17]{0:T(128)} %add_convert_fusion.fresh, s32[8]{0:T(128)} %broadcast_add_fusion.last, bf16[4,16,8,2048]{3,2,1,0:T(8,128)(2,1)} %get-tuple-element.7.got_ref, f32[16,8,128]{2,1,0:T(8,128)} %get-tuple-element.8.stats_ref), custom_call_target="tpu_custom_call" | custom-call | tf_op jit(solution)/shard_map/pallas_call | solution.py:191
  (3 shorter events, 0.0 us)
Async XLA Ops:
  0.0 3.9 %copy-start = (bf16[8,8,8192]{2,1,0:T(8,128)(2,1)S(1)}, bf16[8,8,8192]{2,1,0:T(8,128)(2,1)}, u32[]{:S(2)}) copy-start(bf16[8,8,8192]{2,1,0:T(8,128)(2,1)} %param.4) | copy-start | bytes 3145732

commit v2 on v1

v2 whole, which is shorter than its diff:
```python
import functools

import jax
import jax.numpy as jnp
from jax import lax
from jax.experimental import pallas as pl
from jax.experimental.pallas import tpu as pltpu
from jax.sharding import PartitionSpec as P

HEAD_DIM = 128
CHUNKS = 4


def attend_kernel(
    peers, counts, doc_ids, q_hbm, kv_hbm, out_hbm,
    raw_buf, doc_buf, send_buf, q_buf, o_buf, got_buf, s_buf, stats_buf, w_buf, top_buf,
    run_buf, out_buf, kv_buf, ends, page_doc, page_block, fresh,
    raw_sem, q_send, q_recv, o_send, o_recv, s_send, s_recv, own_q_sem, own_o_sem, own_s_sem,
    kv_sem, out_sem,
):
    chunks, _, rows, wide = q_buf.shape
    blocks = counts.shape[0]
    me = lax.axis_index("ctx")
    tokens = peers * rows
    heads_chunk = wide // HEAD_DIM
    kv_heads = kv_buf.shape[2] // HEAD_DIM
    groups = chunks * heads_chunk // kv_heads
    mesh_id = pl.DeviceIdType.MESH

    barrier = pltpu.get_barrier_semaphore()

    @pl.loop(1, peers)
    def _(k):
        pl.semaphore_signal(
            barrier, inc=1, device_id={"ctx": lax.rem(me + k, peers)}, device_id_type=mesh_id
        )

    def columns(c):
        return pl.ds(c * wide, wide)

    raw_copies = [
        pltpu.make_async_copy(q_hbm.at[:, :, columns(c)], raw_buf.at[c], raw_sem.at[c])
        for c in range(chunks)
    ]
    for copy in raw_copies:
        copy.start()
    kv_copy = pltpu.make_async_copy(kv_hbm.at[0], kv_buf, kv_sem)
    kv_copy.start()

    end = 0
    for j in range(blocks):
        end = end + counts[j]
        ends[j] = end

    def locate(n, before):
        doc = 0
        for j in range(blocks):
            doc = doc + (n >= ends[j]).astype(jnp.int32)
        block = 0
        for j in range(1, blocks):
            block = block + jnp.where(doc_ids[j] == doc, j, 0)
        page_doc[n] = doc
        page_block[n] = block
        fresh[n] = (doc != before).astype(jnp.int32)
        return doc

    lax.fori_loop(0, peers, locate, jnp.int32(-1))
    fresh[peers] = 1

    def send(src, dst, send_sem, recv_sem):
        @pl.loop(1, peers)
        def _(k):
            peer = lax.rem(me + k, peers)
            pltpu.make_async_remote_copy(
                src_ref=src.at[peer], dst_ref=dst.at[me], send_sem=send_sem,
                recv_sem=recv_sem, device_id={"ctx": peer}, device_id_type=mesh_id,
            ).start()

    def drain(ref, sem):
        part = ref.at[pl.ds(0, peers - 1)]
        pltpu.make_async_copy(part, part, sem).wait()

    own_q, own_o = [], []
    for c in range(chunks):
        raw_copies[c].wait()
        raw = raw_buf[c].astype(jnp.float32)
        doc_buf[c] = jnp.swapaxes(raw, 0, 1).astype(jnp.bfloat16)

        @pl.loop(0, peers)
        def _(n):
            send_buf[c, n] = doc_buf[c, page_block[n]]

        if c == 0:
            pl.semaphore_wait(barrier, peers - 1)
        send(send_buf.at[c], q_buf.at[c], q_send.at[c], q_recv.at[c])
        copy = pltpu.make_async_copy(send_buf.at[c, me], q_buf.at[c, me], own_q_sem.at[c])
        copy.start()
        own_q.append(copy)

    s_buf[...] = jnp.zeros_like(s_buf)
    kv_copy.wait()
    lane = lax.broadcasted_iota(jnp.int32, (tokens, 128), 1)
    own_s = pltpu.make_async_copy(s_buf.at[me], stats_buf.at[me], own_s_sem)
    for c in range(chunks):
        own_q[c].wait()
        drain(q_buf.at[c], q_recv.at[c])

        def head(j, carry):
            lanes = pl.ds(pl.multiple_of(j * HEAD_DIM, HEAD_DIM), HEAD_DIM)
            h = c * heads_chunk + j
            kv_lanes = pl.ds(pl.multiple_of(h // groups * HEAD_DIM, HEAD_DIM), HEAD_DIM)
            q = q_buf[c, :, :, lanes].astype(jnp.float32).reshape(tokens, HEAD_DIM)
            s = lax.dot_general(
                q.astype(jnp.bfloat16), kv_buf[0, :, kv_lanes], (((1,), (1,)), ((), ())),
                preferred_element_type=jnp.float32,
            ) * HEAD_DIM ** (-0.5)
            top = jnp.max(s, axis=-1, keepdims=True)
            p = jnp.exp(s - top)
            total = jnp.sum(p, axis=-1, keepdims=True)
            o = jnp.dot(
                p.astype(jnp.bfloat16), kv_buf[1, :, kv_lanes],
                preferred_element_type=jnp.float32,
            ) / total
            o_buf[c, :, :, lanes] = o.reshape(peers, rows, HEAD_DIM).astype(jnp.bfloat16)
            old = s_buf[...].reshape(tokens, 128)
            new = jnp.where(lane == h, top, jnp.where(lane == h + 64, total, old))
            s_buf[...] = new.reshape(peers, rows, 128)
            return carry

        lax.fori_loop(0, heads_chunk, head, 0)
        if c == chunks - 1:
            send(s_buf, stats_buf, s_send, s_recv)
            own_s.start()
        send(o_buf.at[c], got_buf.at[c], o_send.at[c], o_recv.at[c])
        copy = pltpu.make_async_copy(o_buf.at[c, me], got_buf.at[c, me], own_o_sem.at[c])
        copy.start()
        own_o.append(copy)

    own_s.wait()
    drain(stats_buf, s_recv)

    def forward(n, top):
        mine = stats_buf[n]
        top = jnp.where(fresh[n] == 1, mine, jnp.maximum(top, mine))
        top_buf[n] = top
        return top

    def backward(i, top):
        n = peers - 1 - i
        top = jnp.where(fresh[n + 1] == 1, top_buf[n], top)
        top_buf[n] = top
        return top

    def weigh(n, total):
        mine = stats_buf[n]
        w = jnp.exp(mine - top_buf[n]) * pltpu.roll(mine, 128 - 64, 1)
        w_buf[n] = w
        total = jnp.where(fresh[n] == 1, w, total + w)
        top_buf[n] = total
        return total

    def norm(i, total):
        n = peers - 1 - i
        total = jnp.where(fresh[n + 1] == 1, top_buf[n], total)
        w_buf[n] = w_buf[n] / total
        return total

    zero = jnp.zeros((rows, 128), jnp.float32)
    lax.fori_loop(0, peers, forward, zero)
    lax.fori_loop(0, peers, backward, zero)
    lax.fori_loop(0, peers, weigh, zero)
    lax.fori_loop(0, peers, norm, zero)

    outs = []
    for c in range(chunks):
        own_o[c].wait()
        drain(got_buf.at[c], o_recv.at[c])

        def visit(n, acc):
            w = w_buf[n]
            w = jnp.concatenate(
                [
                    jnp.broadcast_to(w[:, h:h + 1], (rows, HEAD_DIM))
                    for h in range(c * heads_chunk, (c + 1) * heads_chunk)
                ],
                axis=1,
            )
            mine = w * got_buf[c, n].astype(jnp.float32)
            acc = jnp.where(fresh[n] == 1, mine, acc + mine)
            run_buf[n] = acc
            return acc

        lax.fori_loop(0, peers, visit, jnp.zeros((rows, wide), jnp.float32), unroll=2)
        picked = jnp.stack([run_buf[jnp.clip(ends[doc_ids[b]] - 1, 0, peers - 1)] for b in range(blocks)], axis=0)
        out_buf[c] = jnp.swapaxes(picked, 0, 1).astype(jnp.bfloat16)
        copy = pltpu.make_async_copy(out_buf.at[c], out_hbm.at[:, :, columns(c)], out_sem.at[c])
        copy.start()
        outs.append(copy)
    drain(s_buf, s_send)
    for c in range(chunks):
        drain(send_buf.at[c], q_send.at[c])
        drain(o_buf.at[c], o_send.at[c])
        outs[c].wait()


def body(queries, kv_cache, page_counts, doc_ids):
    peers = lax.axis_size("ctx")
    rows, blocks, width = queries.shape
    assert kv_cache.shape[0] == 1 and width == 64 * HEAD_DIM
    wide = width // CHUNKS
    any_spec = pl.BlockSpec(memory_space=pl.ANY)
    smem_spec = pl.BlockSpec(memory_space=pltpu.SMEM)
    dma = pltpu.SemaphoreType.DMA
    pieces = pltpu.VMEM((CHUNKS, peers, rows, wide), jnp.bfloat16)
    stats = pltpu.VMEM((peers, rows, 128), jnp.float32)
    return pl.pallas_call(
        functools.partial(attend_kernel, peers),
        out_shape=jax.ShapeDtypeStruct(queries.shape, jnp.bfloat16),
        in_specs=[smem_spec, smem_spec, any_spec, any_spec],
        out_specs=any_spec,
        scratch_shapes=[
            pltpu.VMEM((CHUNKS, rows, blocks, wide), jnp.bfloat16),
            pltpu.VMEM((CHUNKS, blocks, rows, wide), jnp.bfloat16),
            pieces, pieces, pieces, pieces,
            stats, stats, stats, stats,
            pltpu.VMEM((peers, rows, wide), jnp.float32),
            pltpu.VMEM((CHUNKS, rows, blocks, wide), jnp.bfloat16),
            pltpu.VMEM(kv_cache.shape[1:], jnp.bfloat16),
            pltpu.SMEM((blocks,), jnp.int32),
            pltpu.SMEM((peers,), jnp.int32),
            pltpu.SMEM((peers,), jnp.int32),
            pltpu.SMEM((peers + 1,), jnp.int32),
            dma((CHUNKS,)),
            dma((CHUNKS,)), dma((CHUNKS,)), dma((CHUNKS,)), dma((CHUNKS,)),
            dma(()), dma(()), dma((CHUNKS,)), dma((CHUNKS,)), dma(()),
            dma(()), dma((CHUNKS,)),
        ],
        compiler_params=pltpu.CompilerParams(collective_id=0, has_side_effects=True),
    )(page_counts, doc_ids, queries, kv_cache)


def solution(mesh):
    placed = (
        P(("group", "ctx"), None, None),
        P(("group", "ctx"), None, None, None),
        P("group"),
        P("group"),
    )
    return jax.shard_map(
        body, mesh=mesh, in_specs=placed, out_specs=P(("group", "ctx"), None, None), check_vma=False
    )
```

time: 129 us -> 104 us (0.81)
  local copies, waits for them, and re-layouts: 11.2 us -> 2.26 us
  Pallas kernels: 108 us -> 99.4 us
  other arithmetic: 7.57 us -> 0 us
    gather x2 -> x0, local copies, waits for them, and re-layouts: 11.2 us -> none  [body(): outgoing = jnp.take(queries, page_blocks, axis=1)]
    pallas_call x2 -> x1, Pallas kernels: 108 us -> 99.4 us  [body(): pl.pallas_call(functools.partial(attend_kernel, peers), out_shape=jax.Sha...]
    transpose x1 -> x0, other arithmetic: 3.73 us -> none  [body(): outgoing.reshape(rows, peers, CHUNKS, width // CHUNKS).transpose(2, 1, 0, 3)]
    unnamed x2 -> x1, local copies, waits for them, and re-layouts: 0.01 us -> 2.26 us
    reduce_sum x3 -> x0, other arithmetic: 1.66 us -> none  [the longest x1 0.84 us: body(): jnp.sum(jnp.where(doc_ids[:, None] == block_order[None, :], doc_ends[None...]
where the time goes in v2:
time: 104 us; the launch traced here: 102 us
  Pallas kernels  99.4 us (96%)
  local copies, waits for them, and re-layouts  2.26 us (2%)
    pallas_call x1, Pallas kernels, body(): pl.pallas_call(functools.partial(attend_kernel, peers), out_shape=jax.Sha...  99.4 us
    unnamed x1, local copies, waits for them, and re-layouts  2.26 us

profile of v2, /device:TPU:15, one launch (start us, length us, event | category | flops | bytes accessed | tf_op | source)
XLA Modules:
  0.0 101.7 jit_solution(10026708081868214510)
XLA Ops:
  0.0 99.4 %shard_map.46 = bf16[8,8,8192]{2,1,0:T(8,128)(2,1)} custom-call(s32[8]{0:T(128)} %counts.1, s32[8]{0:T(128)} %doc_ids.1, bf16[8,8,8192]{2,1,0:T(8,128)(2,1)} %q_hbm.1, bf16[1,2,512,1024]{3,2,1,0:T(8,128)(2,1)} %kv_hbm.1), custom_call_target="tpu_custom_call" | custom-call | tf_op jit(solution)/shard_map/pallas_call | solution.py:216
  99.4 2.3 %copy.6 = bf16[8,8,8192]{2,1,0:T(8,128)(2,1)} copy(bf16[8,8,8192]{2,1,0:T(8,128)(2,1)} %shard_map.46) | data formatting | bytes 2097152

commit v3 on v2

--- a/solution.py
+++ b/solution.py
@@ -8,7 +8,7 @@
 from jax.sharding import PartitionSpec as P
 
 HEAD_DIM = 128
-CHUNKS = 4
+CHUNKS = 8
 
 
 def attend_kernel(

time: 104 us -> 109 us (1.048)
  Pallas kernels: 99.4 us -> 104 us
    pallas_call x1, Pallas kernels: 99.4 us -> 104 us  [body(): pl.pallas_call(functools.partial(attend_kernel, peers), out_shape=jax.Sha...]
where the time goes in v3:
time: 109 us; the launch traced here: 106 us
  Pallas kernels  104 us (95%)
  local copies, waits for them, and re-layouts  2.26 us (2%)
    pallas_call x1, Pallas kernels, body(): pl.pallas_call(functools.partial(attend_kernel, peers), out_shape=jax.Sha...  104 us
    unnamed x1, local copies, waits for them, and re-layouts  2.26 us

profile of v3, /device:TPU:15, one launch (start us, length us, event | category | flops | bytes accessed | tf_op | source)
XLA Modules:
  0.0 106.4 jit_solution(13199233377775536238)
XLA Ops:
  0.0 104.1 %shard_map.46 = bf16[8,8,8192]{2,1,0:T(8,128)(2,1)} custom-call(s32[8]{0:T(128)} %counts.1, s32[8]{0:T(128)} %doc_ids.1, bf16[8,8,8192]{2,1,0:T(8,128)(2,1)} %q_hbm.1, bf16[1,2,512,1024]{3,2,1,0:T(8,128)(2,1)} %kv_hbm.1), custom_call_target="tpu_custom_call" | custom-call | tf_op jit(solution)/shard_map/pallas_call | solution.py:216
  104.1 2.3 %copy.6 = bf16[8,8,8192]{2,1,0:T(8,128)(2,1)} copy(bf16[8,8,8192]{2,1,0:T(8,128)(2,1)} %shard_map.46) | data formatting | bytes 2097152

commit v4 on v2

--- a/solution.py
+++ b/solution.py
@@ -9,16 +9,18 @@
 
 HEAD_DIM = 128
 CHUNKS = 4
+Q_CHUNKS = 4
 
 
 def attend_kernel(
-    peers, counts, doc_ids, q_hbm, kv_hbm, out_hbm,
+    peers, counts, doc_ids, q_hbm, kv_hbm, out_ref,
     raw_buf, doc_buf, send_buf, q_buf, o_buf, got_buf, s_buf, stats_buf, w_buf, top_buf,
-    run_buf, out_buf, kv_buf, ends, page_doc, page_block, fresh,
+    run_buf, wide_buf, kv_buf, ends, page_doc, page_block, fresh,
     raw_sem, q_send, q_recv, o_send, o_recv, s_send, s_recv, own_q_sem, own_o_sem, own_s_sem,
-    kv_sem, out_sem,
+    kv_sem,
 ):
-    chunks, _, rows, wide = q_buf.shape
+    chunks, _, rows, wide = o_buf.shape
+    q_chunks, _, _, q_wide = q_buf.shape
     blocks = counts.shape[0]
     me = lax.axis_index("ctx")
     tokens = peers * rows
@@ -35,12 +37,11 @@
             barrier, inc=1, device_id={"ctx": lax.rem(me + k, peers)}, device_id_type=mesh_id
         )
 
-    def columns(c):
-        return pl.ds(c * wide, wide)
-
     raw_copies = [
-        pltpu.make_async_copy(q_hbm.at[:, :, columns(c)], raw_buf.at[c], raw_sem.at[c])
-        for c in range(chunks)
+        pltpu.make_async_copy(
+            q_hbm.at[:, :, pl.ds(c * q_wide, q_wide)], raw_buf.at[c], raw_sem.at[c]
+        )
+        for c in range(q_chunks)
     ]
     for copy in raw_copies:
         copy.start()
@@ -81,7 +82,7 @@
         pltpu.make_async_copy(part, part, sem).wait()
 
     own_q, own_o = [], []
-    for c in range(chunks):
+    for c in range(q_chunks):
         raw_copies[c].wait()
         raw = raw_buf[c].astype(jnp.float32)
         doc_buf[c] = jnp.swapaxes(raw, 0, 1).astype(jnp.bfloat16)
@@ -102,14 +103,17 @@
     lane = lax.broadcasted_iota(jnp.int32, (tokens, 128), 1)
     own_s = pltpu.make_async_copy(s_buf.at[me], stats_buf.at[me], own_s_sem)
     for c in range(chunks):
-        own_q[c].wait()
-        drain(q_buf.at[c], q_recv.at[c])
+        piece, offset = divmod(c * wide, q_wide)
+        if offset == 0:
+            own_q[piece].wait()
+            drain(q_buf.at[piece], q_recv.at[piece])
 
         def head(j, carry):
             lanes = pl.ds(pl.multiple_of(j * HEAD_DIM, HEAD_DIM), HEAD_DIM)
             h = c * heads_chunk + j
             kv_lanes = pl.ds(pl.multiple_of(h // groups * HEAD_DIM, HEAD_DIM), HEAD_DIM)
-            q = q_buf[c, :, :, lanes].astype(jnp.float32).reshape(tokens, HEAD_DIM)
+            q_lanes = pl.ds(pl.multiple_of(offset + j * HEAD_DIM, HEAD_DIM), HEAD_DIM)
+            q = q_buf[piece, :, :, q_lanes].astype(jnp.float32).reshape(tokens, HEAD_DIM)
             s = lax.dot_general(
                 q.astype(jnp.bfloat16), kv_buf[0, :, kv_lanes], (((1,), (1,)), ((), ())),
                 preferred_element_type=jnp.float32,
@@ -171,36 +175,34 @@
     lax.fori_loop(0, peers, weigh, zero)
     lax.fori_loop(0, peers, norm, zero)
 
-    outs = []
     for c in range(chunks):
+
+        @pl.loop(0, peers)
+        def _(n):
+            w = w_buf[n]
+            for i in range(heads_chunk):
+                h = c * heads_chunk + i
+                wide_buf[n, :, i * HEAD_DIM:(i + 1) * HEAD_DIM] = jnp.broadcast_to(
+                    w[:, h:h + 1], (rows, HEAD_DIM)
+                )
+
         own_o[c].wait()
         drain(got_buf.at[c], o_recv.at[c])
 
         def visit(n, acc):
-            w = w_buf[n]
-            w = jnp.concatenate(
-                [
-                    jnp.broadcast_to(w[:, h:h + 1], (rows, HEAD_DIM))
-                    for h in range(c * heads_chunk, (c + 1) * heads_chunk)
-                ],
-                axis=1,
-            )
-            mine = w * got_buf[c, n].astype(jnp.float32)
+            mine = wide_buf[n] * got_buf[c, n].astype(jnp.float32)
             acc = jnp.where(fresh[n] == 1, mine, acc + mine)
             run_buf[n] = acc
             return acc
 
         lax.fori_loop(0, peers, visit, jnp.zeros((rows, wide), jnp.float32), unroll=2)
         picked = jnp.stack([run_buf[jnp.clip(ends[doc_ids[b]] - 1, 0, peers - 1)] for b in range(blocks)], axis=0)
-        out_buf[c] = jnp.swapaxes(picked, 0, 1).astype(jnp.bfloat16)
-        copy = pltpu.make_async_copy(out_buf.at[c], out_hbm.at[:, :, columns(c)], out_sem.at[c])
-        copy.start()
-        outs.append(copy)
+        out_ref[:, :, c * wide:(c + 1) * wide] = jnp.swapaxes(picked, 0, 1).astype(jnp.bfloat16)
     drain(s_buf, s_send)
+    for c in range(q_chunks):
+        drain(send_buf.at[c], q_send.at[c])
     for c in range(chunks):
-        drain(send_buf.at[c], q_send.at[c])
         drain(o_buf.at[c], o_send.at[c])
-        outs[c].wait()
 
 
 def body(queries, kv_cache, page_counts, doc_ids):
@@ -208,34 +210,36 @@
     rows, blocks, width = queries.shape
     assert kv_cache.shape[0] == 1 and width == 64 * HEAD_DIM
     wide = width // CHUNKS
-    any_spec = pl.BlockSpec(memory_space=pl.ANY)
+    q_wide = width // Q_CHUNKS
+    hbm_spec = pl.BlockSpec(memory_space=pltpu.HBM)
     smem_spec = pl.BlockSpec(memory_space=pltpu.SMEM)
     dma = pltpu.SemaphoreType.DMA
+    q_pieces = pltpu.VMEM((Q_CHUNKS, peers, rows, q_wide), jnp.bfloat16)
     pieces = pltpu.VMEM((CHUNKS, peers, rows, wide), jnp.bfloat16)
     stats = pltpu.VMEM((peers, rows, 128), jnp.float32)
     return pl.pallas_call(
         functools.partial(attend_kernel, peers),
         out_shape=jax.ShapeDtypeStruct(queries.shape, jnp.bfloat16),
-        in_specs=[smem_spec, smem_spec, any_spec, any_spec],
-        out_specs=any_spec,
+        in_specs=[smem_spec, smem_spec, hbm_spec, hbm_spec],
+        out_specs=pl.BlockSpec(memory_space=pltpu.VMEM),
         scratch_shapes=[
-            pltpu.VMEM((CHUNKS, rows, blocks, wide), jnp.bfloat16),
-            pltpu.VMEM((CHUNKS, blocks, rows, wide), jnp.bfloat16),
-            pieces, pieces, pieces, pieces,
+            pltpu.VMEM((Q_CHUNKS, rows, blocks, q_wide), jnp.bfloat16),
+            pltpu.VMEM((Q_CHUNKS, blocks, rows, q_wide), jnp.bfloat16),
+            q_pieces, q_pieces, pieces, pieces,
             stats, stats, stats, stats,
             pltpu.VMEM((peers, rows, wide), jnp.float32),
-            pltpu.VMEM((CHUNKS, rows, blocks, wide), jnp.bfloat16),
+            pltpu.VMEM((peers, rows, wide), jnp.float32),
             pltpu.VMEM(kv_cache.shape[1:], jnp.bfloat16),
             pltpu.SMEM((blocks,), jnp.int32),
             pltpu.SMEM((peers,), jnp.int32),
             pltpu.SMEM((peers,), jnp.int32),
             pltpu.SMEM((peers + 1,), jnp.int32),
-            dma((CHUNKS,)),
-            dma((CHUNKS,)), dma((CHUNKS,)), dma((CHUNKS,)), dma((CHUNKS,)),
-            dma(()), dma(()), dma((CHUNKS,)), dma((CHUNKS,)), dma(()),
-            dma(()), dma((CHUNKS,)),
+            dma((Q_CHUNKS,)),
+            dma((Q_CHUNKS,)), dma((Q_CHUNKS,)), dma((CHUNKS,)), dma((CHUNKS,)),
+            dma(()), dma(()), dma((Q_CHUNKS,)), dma((CHUNKS,)), dma(()),
+            dma(()),
         ],
-        compiler_params=pltpu.CompilerParams(collective_id=0, has_side_effects=True),
+        compiler_params=pltpu.CompilerParams(collective_id=0, has_side_effects=True, vmem_limit_bytes=32 << 20),
     )(page_counts, doc_ids, queries, kv_cache)
 
 

time: 104 us -> 108 us (1.038)
  the two profiles are of different devices: /device:TPU:15 before, /device:TPU:0 now
where the time goes in v4:
time: 108 us
  Pallas kernels  103 us (95%)
  local copies, waits for them, and re-layouts  5.1 us (5%)
    pallas_call x1, Pallas kernels, body(): pl.pallas_call(functools.partial(attend_kernel, peers), out_shape=jax.Sha...  103 us
    unnamed x9, local copies, waits for them, and re-layouts  5.1 us

profile of v4, /device:TPU:0, one launch (start us, length us, event | category | flops | bytes accessed | tf_op | source)
XLA Modules:
  0.0 108.1 jit_solution(2177598316374975803)
XLA Ops:
  0.0 0.0 copy-start
  0.0 1.6 %copy-done = bf16[1,2,512,1024]{3,2,1,0:T(8,128)(2,1)S(1)} copy-done((bf16[1,2,512,1024]{3,2,1,0:T(8,128)(2,1)S(1)}, bf16[1,2,512,1024]{3,2,1,0:T(8,128)(2,1)}, u32[]{:S(2)}) %copy-start) | copy-done | bytes 2097176
  1.6 0.0 copy-start.1
  1.6 1.2 %copy-done.1 = bf16[8,8,8192]{2,1,0:T(8,128)(2,1)S(1)} copy-done((bf16[8,8,8192]{2,1,0:T(8,128)(2,1)S(1)}, bf16[8,8,8192]{2,1,0:T(8,128)(2,1)}, u32[]{:S(2)}) %copy-start.1) | copy-done | bytes 1048600
  2.8 0.0 copy-start.2
  2.8 0.7 copy-done.2
  3.5 0.0 copy-start.3
  3.5 0.7 copy-done.3
  4.1 103.0 %shard_map.46 = bf16[8,8,8192]{2,1,0:T(8,128)(2,1)S(1)} custom-call(s32[8]{0:T(128)S(1)} %copy-done.2, s32[8]{0:T(128)S(1)} %copy-done.3, bf16[8,8,8192]{2,1,0:T(8,128)(2,1)S(1)} %copy-done.1, bf16[1,2,512,1024]{3,2,1,0:T(8,128)(2,1)S(1)} %copy-done), custom_call_target="tpu_custom_call" | custom-call | tf_op jit(solution)/shard_map/pallas_call | solution.py:220
  107.1 1.0 copy.6
Async XLA Ops:
  0.0 1.6 %copy-start = (bf16[1,2,512,1024]{3,2,1,0:T(8,128)(2,1)S(1)}, bf16[1,2,512,1024]{3,2,1,0:T(8,128)(2,1)}, u32[]{:S(2)}) copy-start(bf16[1,2,512,1024]{3,2,1,0:T(8,128)(2,1)} %kv_hbm.1) | copy-start | bytes 6291460
  1.6 1.2 %copy-start.1 = (bf16[8,8,8192]{2,1,0:T(8,128)(2,1)S(1)}, bf16[8,8,8192]{2,1,0:T(8,128)(2,1)}, u32[]{:S(2)}) copy-start(bf16[8,8,8192]{2,1,0:T(8,128)(2,1)} %q_hbm.1) | copy-start | bytes 3145732
  2.8 0.7 copy-start.2
  3.5 0.7 copy-start.3

commit v5 on v4

--- a/solution.py
+++ b/solution.py
@@ -13,11 +13,11 @@
 
 
 def attend_kernel(
-    peers, counts, doc_ids, q_hbm, kv_hbm, out_ref,
+    peers, counts, doc_ids, q_hbm, kv_hbm, out_hbm,
     raw_buf, doc_buf, send_buf, q_buf, o_buf, got_buf, s_buf, stats_buf, w_buf, top_buf,
-    run_buf, wide_buf, kv_buf, ends, page_doc, page_block, fresh,
+    run_buf, wide_buf, out_buf, kv_buf, ends, page_doc, page_block, fresh,
     raw_sem, q_send, q_recv, o_send, o_recv, s_send, s_recv, own_q_sem, own_o_sem, own_s_sem,
-    kv_sem,
+    kv_sem, out_sem,
 ):
     chunks, _, rows, wide = o_buf.shape
     q_chunks, _, _, q_wide = q_buf.shape
@@ -135,7 +135,8 @@
         if c == chunks - 1:
             send(s_buf, stats_buf, s_send, s_recv)
             own_s.start()
-        send(o_buf.at[c], got_buf.at[c], o_send.at[c], o_recv.at[c])
+        for i in {0: [0], chunks - 1: range(1, chunks)}.get(c, []):
+            send(o_buf.at[i], got_buf.at[i], o_send.at[i], o_recv.at[i])
         copy = pltpu.make_async_copy(o_buf.at[c, me], got_buf.at[c, me], own_o_sem.at[c])
         copy.start()
         own_o.append(copy)
@@ -175,6 +176,7 @@
     lax.fori_loop(0, peers, weigh, zero)
     lax.fori_loop(0, peers, norm, zero)
 
+    outs = []
     for c in range(chunks):
 
         @pl.loop(0, peers)
@@ -197,12 +199,18 @@
 
         lax.fori_loop(0, peers, visit, jnp.zeros((rows, wide), jnp.float32), unroll=2)
         picked = jnp.stack([run_buf[jnp.clip(ends[doc_ids[b]] - 1, 0, peers - 1)] for b in range(blocks)], axis=0)
-        out_ref[:, :, c * wide:(c + 1) * wide] = jnp.swapaxes(picked, 0, 1).astype(jnp.bfloat16)
+        out_buf[c] = jnp.swapaxes(picked, 0, 1).astype(jnp.bfloat16)
+        copy = pltpu.make_async_copy(
+            out_buf.at[c], out_hbm.at[:, :, pl.ds(c * wide, wide)], out_sem.at[c]
+        )
+        copy.start()
+        outs.append(copy)
     drain(s_buf, s_send)
     for c in range(q_chunks):
         drain(send_buf.at[c], q_send.at[c])
     for c in range(chunks):
         drain(o_buf.at[c], o_send.at[c])
+        outs[c].wait()
 
 
 def body(queries, kv_cache, page_counts, doc_ids):
@@ -221,7 +229,7 @@
         functools.partial(attend_kernel, peers),
         out_shape=jax.ShapeDtypeStruct(queries.shape, jnp.bfloat16),
         in_specs=[smem_spec, smem_spec, hbm_spec, hbm_spec],
-        out_specs=pl.BlockSpec(memory_space=pltpu.VMEM),
+        out_specs=pl.BlockSpec(memory_space=pl.ANY),
         scratch_shapes=[
             pltpu.VMEM((Q_CHUNKS, rows, blocks, q_wide), jnp.bfloat16),
             pltpu.VMEM((Q_CHUNKS, blocks, rows, q_wide), jnp.bfloat16),
@@ -229,6 +237,7 @@
             stats, stats, stats, stats,
             pltpu.VMEM((peers, rows, wide), jnp.float32),
             pltpu.VMEM((peers, rows, wide), jnp.float32),
+            pltpu.VMEM((CHUNKS, rows, blocks, wide), jnp.bfloat16),
             pltpu.VMEM(kv_cache.shape[1:], jnp.bfloat16),
             pltpu.SMEM((blocks,), jnp.int32),
             pltpu.SMEM((peers,), jnp.int32),
@@ -237,9 +246,9 @@
             dma((Q_CHUNKS,)),
             dma((Q_CHUNKS,)), dma((Q_CHUNKS,)), dma((CHUNKS,)), dma((CHUNKS,)),
             dma(()), dma(()), dma((Q_CHUNKS,)), dma((CHUNKS,)), dma(()),
-            dma(()),
+            dma(()), dma((CHUNKS,)),
         ],
-        compiler_params=pltpu.CompilerParams(collective_id=0, has_side_effects=True, vmem_limit_bytes=32 << 20),
+        compiler_params=pltpu.CompilerParams(collective_id=0, has_side_effects=True),
     )(page_counts, doc_ids, queries, kv_cache)
 
 

time: 108 us -> 104 us (0.963)
  the two profiles are of different devices: /device:TPU:0 before, /device:TPU:15 now
where the time goes in v5:
time: 104 us; the launch traced here: 102 us
  Pallas kernels  100 us (96%)
  local copies, waits for them, and re-layouts  2.26 us (2%)
    pallas_call x1, Pallas kernels, body(): pl.pallas_call(functools.partial(attend_kernel, peers), out_shape=jax.Sha...  100 us
    unnamed x1, local copies, waits for them, and re-layouts  2.26 us

profile of v5, /device:TPU:15, one launch (start us, length us, event | category | flops | bytes accessed | tf_op | source)
XLA Modules:
  0.0 102.4 jit_solution(6502390342465757103)
XLA Ops:
  0.0 100.1 %shard_map.46 = bf16[8,8,8192]{2,1,0:T(8,128)(2,1)} custom-call(s32[8]{0:T(128)} %counts.1, s32[8]{0:T(128)} %doc_ids.1, bf16[8,8,8192]{2,1,0:T(8,128)(2,1)} %q_hbm.1, bf16[1,2,512,1024]{3,2,1,0:T(8,128)(2,1)} %kv_hbm.1), custom_call_target="tpu_custom_call" | custom-call | tf_op jit(solution)/shard_map/pallas_call | solution.py:228
  100.1 2.3 %copy.6 = bf16[8,8,8192]{2,1,0:T(8,128)(2,1)} copy(bf16[8,8,8192]{2,1,0:T(8,128)(2,1)} %shard_map.46) | data formatting | bytes 2097152
